TPU v7x, 32 devices: a whole 2x2x4 slice. The times are simulated.
32 devices in a mesh: groups: 2 (over x), dp: 16 (over z, y, core).
Axes of the slice: x: 2, y: 2, z: 4, core: 2. Of those that a mesh axis runs over, the one named last changes fastest.
Arguments:
- activations: bfloat16 [12288, 16384], P(('groups', 'dp')), parts along dimension 0, may hold values from -18 to 18
- labels: int32 [12288], P(('groups', 'dp')), parts along dimension 0, may hold values from 0 to 63, as said below
- counts: int32 [12288], P(('groups', 'dp')), parts along dimension 0, may hold values from 1 to 4
Outputs:
- solution: float32 [32768, 64], P(('groups', 'dp')), parts along dimension 0
- residual: float32 [32768, 64], P(('groups', 'dp')), parts along dimension 0
There are 2 independent parts, one for each index of `groups`. A program takes and returns all parts, laid end to end along the dimension named above; each array names one. Nothing has to cross between parts.
Inputs may be any that keep to these rules, and one draw needn't show every extreme that they name: `labels`: concept index of each row; every concept of 0 to 63 names at least one row. `counts`: integer sample weight of each row.
All inputs are finite; a program needn't handle non-finite values.
Results may differ from a plain program's by a relative error of at most 0.012.
The roundings to bfloat16 on the way count: a program that leaves them out, or rounds other values in their place, can miss the bound.
Values may be sent and summed in bfloat16 or wider, within the bound.
No kernel may reach another device: no remote copies, remote signals or barrier semaphores. Data moves between devices by JAX's collectives and lax.ppermute only.
A program may use at most 64 MiB of HBM per device.

v0:
```python
import jax
import jax.numpy as jnp
from jax import lax
from jax.sharding import PartitionSpec as P

K = 64
ITERS = 2
RIDGE = 0.1


def precise(left_side, right_side):
    return jnp.dot(
        left_side, right_side, precision=lax.Precision.HIGHEST, preferred_element_type=jnp.float32
    )


def symmetric(matrix):
    return 0.5 * (matrix + matrix.T)


def solve_positive(matrix, target):
    return jax.scipy.linalg.cho_solve((jnp.linalg.cholesky(matrix), True), target)


def contract_rows(left_side, right_side):
    return lax.dot_general(
        left_side, right_side, (((0,), (0,)), ((), ())), preferred_element_type=jnp.float32
    )


def per_device(activations, labels, counts):
    weights = counts.astype(jnp.float32)
    classes = jnp.arange(K, dtype=jnp.int32)
    member_full = jnp.where(labels[:, None] == classes[None, :], weights[:, None], jnp.float32(0.0))
    local_weight = jnp.sum(member_full, axis=0)
    member = member_full.astype(jnp.bfloat16)
    class_sums = lax.psum_scatter(
        contract_rows(activations, member), "dp", scatter_dimension=0, tiled=True
    )
    class_weight = lax.psum(local_weight, "dp")
    total_weight = jnp.sum(class_weight)
    class_means = class_sums / class_weight[None, :]
    mean_diff = class_means * jnp.sqrt(class_weight)[None, :]
    solution = jnp.zeros_like(mean_diff)
    residual = mean_diff
    direction = mean_diff
    current = symmetric(lax.psum(precise(residual.T, residual), "dp"))
    for iteration in range(ITERS):
        probed = jnp.dot(
            activations,
            lax.all_gather(direction.astype(jnp.bfloat16), "dp", axis=0, tiled=True),
            preferred_element_type=jnp.float32,
        )
        weighted = (weights[:, None] * probed).astype(jnp.bfloat16)
        panel = lax.psum_scatter(
            contract_rows(activations, weighted), "dp", scatter_dimension=0, tiled=True
        )
        cross, along_panel, along_along = lax.psum(
            (
                precise(class_means.T, direction),
                precise(direction.T, panel),
                precise(direction.T, direction),
            ),
            "dp",
        )
        scaled = class_weight[:, None] * cross
        curvature = symmetric(
            (along_panel - precise(cross.T, scaled)) / total_weight + RIDGE * along_along
        )
        step_alpha = solve_positive(curvature, current)
        image = (panel - precise(class_means, scaled)) / total_weight + RIDGE * direction
        solution = solution + precise(direction, step_alpha)
        residual = residual - precise(image, step_alpha)
        renewed = current
        if iteration + 1 < ITERS:
            renewed = symmetric(lax.psum(precise(residual.T, residual), "dp"))
        if iteration + 1 < ITERS:
            step_beta = solve_positive(current, renewed)
            direction = residual + precise(direction, step_beta)
            current = renewed
    return (solution, residual)


def solution(mesh):
    in_specs = (P(("groups", "dp"), None), P(("groups", "dp")), P(("groups", "dp")))
    out_specs = (P(("groups", "dp"), None), P(("groups", "dp"), None))
    return jax.shard_map(
        per_device, mesh=mesh, in_specs=in_specs, out_specs=out_specs, check_vma=False
    )
```

profile of v0, /device:TPU:0, one launch (start us, length us, event | category | flops | bytes accessed | tf_op | source)
XLA Modules:
  0.0 587.8 jit_solution(6999212861251710433)
XLA Ops:
  7.2 0.0 reduce-scatter.4.cloned.1.call-start
  7.2 0.7 convert_element_type.20
  7.9 8.9 %convolution_bitcast_fusion.2 = f32[16384,64]{0,1:T(8,128)} fusion(bf16[384,16384]{1,0:T(8,128)(2,1)} %param.6, f32[384]{0:T(512)S(1)} %convert_element_type.20, s32[384]{0:T(512)} %param.7), kind=kOutput, calls=%fused_computation.2 | convolution fusion | flops 805355520 | bytes 16780288 | tf_op jit(solution)/shard_map/dot_general | solution.py:26
  16.8 0.0 all-gather.3.cloned.1.call-start
  16.8 0.1 select_reduce_fusion
  17.0 35.0 %psum.59 = f32[64]{0:T(128)S(1)} all-reduce(f32[64]{0:T(128)S(1)} %select_reduce_fusion), channel_id=1, replica_groups=mesh['groups'=2,'dp'=16] {'dp'}, use_global_device_ids=true, to_apply=%region_2.3 | all-reduce | flops 64 | bytes 512 | tf_op jit(solution)/shard_map/psum | solution.py:40
  52.0 0.6 fusion.62
  52.6 39.5 %reduce-scatter.4.cloned.1.call-done = f32[1024,64]{0,1:T(8,128)} async-done(((f32[16384,64]{0,1:T(8,128)}), f32[1024,64]{0,1:T(8,128)}) %reduce-scatter.4.cloned.1.call-update) | async-done | bytes 262160 | tf_op jit(solution)/shard_map/reduce_scatter | solution.py:37
  92.1 1.7 multiply_convert_fusion
  93.8 0.0 reduce-scatter.6.cloned.1.call-start
  93.9 41.7 %all-gather.3.cloned.1.call-done = bf16[16384,64]{0,1:T(8,128)(2,1)} async-done(((bf16[1024,64]{0,1:T(8,128)(2,1)}), bf16[16384,64]{0,1:T(8,128)(2,1)}) %all-gather.3.cloned.1.call-update) | async-done | bytes 2097168 | tf_op jit(solution)/shard_map/all_gather | solution.py:51
  135.5 18.5 %convolution_bitcast_fusion.1 = f32[16384,64]{0,1:T(8,128)} fusion(bf16[384,16384]{1,0:T(8,128)(2,1)} %param.6, bf16[16384,64]{0,1:T(8,128)(2,1)} %all-gather.3.cloned.1.call-done, f32[384]{0:T(512)S(1)} %convert_element_type.20), kind=kOutput, calls=%fused_computation.1 | convolution fusion | flops 1610661888 | bytes 18875904 | tf_op jit(solution)/shard_map/dot_general | solution.py:26
  154.0 0.0 all-gather.5.cloned.1.call-start
  154.1 0.5 fusion.13
  154.5 0.5 fusion.15
  155.0 70.3 %reduce-scatter.6.cloned.1.call-done = f32[1024,64]{0,1:T(8,128)} async-done(((f32[16384,64]{0,1:T(8,128)}), f32[1024,64]{0,1:T(8,128)}) %reduce-scatter.6.cloned.1.call-update) | async-done | bytes 262160 | tf_op jit(solution)/shard_map/reduce_scatter | solution.py:55
  225.3 1.4 fusion.17
  226.7 59.2 %all-reduce.1 = (f32[64,64]{1,0:T(8,128)S(1)}, f32[64,64]{1,0:T(8,128)S(1)}, f32[64,64]{1,0:T(8,128)S(1)}) all-reduce(f32[64,64]{1,0:T(8,128)S(1)} %fusion.13, f32[64,64]{1,0:T(8,128)S(1)} %fusion.17, f32[64,64]{1,0:T(8,128)S(1)} %fusion.15), channel_id=1, replica_groups=mesh['groups'=2,'dp'=16] {'dp'}, use_global_device_ids=true, to_apply=%region_7.8 | all-reduce | flops 12288 | bytes 98304 | tf_op jit(solution)/shard_map/psum | solution.py:58
  285.9 0.1 copy.19
  286.0 0.1 copy.20
  286.1 5.8 cholesky.70
  292.0 0.6 compare_reduce_fusion.1
  292.6 0.7 fusion.32
  293.3 4.9 custom-call.10
  298.2 0.9 fusion.9
  299.1 0.1 copy.15
  299.2 0.1 copy.17
  299.3 0.1 copy.18
  299.4 5.9 cholesky.59
  305.3 0.6 compare_reduce_fusion.2
  305.9 0.7 fusion.31
  306.6 4.9 custom-call.9
  311.5 0.2 fusion.48
  311.7 0.2 fusion.46
  311.9 2.1 fusion.3
  314.0 0.4 convolution_subtract_fusion.2
  314.4 0.4 fusion.64
  314.8 57.6 %psum.63 = f32[64,64]{1,0:T(8,128)S(1)} all-reduce(f32[64,64]{1,0:T(8,128)S(1)} %fusion.64), channel_id=1, replica_groups=mesh['groups'=2,'dp'=16] {'dp'}, use_global_device_ids=true, to_apply=%region_10.13 | all-reduce | flops 4096 | bytes 32768 | tf_op jit(solution)/shard_map/psum | solution.py:76
  372.4 0.1 copy.21
  372.5 0.2 fusion.42
  372.8 0.2 fusion.40
  372.9 1.1 fusion.63
  374.1 0.3 reduce-scatter.8.cloned.1.call-start
  374.3 38.6 %all-gather.5.cloned.1.call-done = bf16[16384,64]{0,1:T(8,128)(2,1)} async-done(((bf16[1024,64]{0,1:T(8,128)(2,1)}), bf16[16384,64]{0,1:T(8,128)(2,1)}) %all-gather.5.cloned.1.call-update) | async-done | bytes 2097168 | tf_op jit(solution)/shard_map/all_gather | solution.py:51
  412.9 18.5 %convolution_bitcast_fusion = f32[16384,64]{0,1:T(8,128)} fusion(bf16[384,16384]{1,0:T(8,128)(2,1)} %param.6, bf16[16384,64]{0,1:T(8,128)(2,1)} %all-gather.5.cloned.1.call-done, f32[384]{0:T(512)S(1)} %convert_element_type.20), kind=kOutput, calls=%fused_computation | convolution fusion | flops 1610661888 | bytes 18875904 | tf_op jit(solution)/shard_map/dot_general | solution.py:26
  431.4 0.4 fusion.66
  431.7 0.4 fusion.61
  432.2 0.5 fusion.11
  432.6 70.1 %reduce-scatter.8.cloned.1.call-done = f32[1024,64]{0,1:T(8,128)} async-done(((f32[16384,64]{0,1:T(8,128)}), f32[1024,64]{0,1:T(8,128)}) %reduce-scatter.8.cloned.1.call-update) | async-done | bytes 262160 | tf_op jit(solution)/shard_map/reduce_scatter | solution.py:55
  502.8 1.3 fusion.65
  504.1 59.1 %all-reduce = (f32[64,64]{1,0:T(8,128)S(1)}, f32[64,64]{1,0:T(8,128)S(1)}, f32[64,64]{1,0:T(8,128)S(1)}) all-reduce(f32[64,64]{1,0:T(8,128)S(1)} %fusion.65, f32[64,64]{1,0:T(8,128)S(1)} %fusion.61, f32[64,64]{1,0:T(8,128)S(1)} %fusion.66), channel_id=1, replica_groups=mesh['groups'=2,'dp'=16] {'dp'}, use_global_device_ids=true, to_apply=%region_12.15 | all-reduce | flops 12288 | bytes 98304 | tf_op jit(solution)/shard_map/psum | solution.py:58
  563.2 0.9 fusion.7
  564.1 0.1 copy.22
  564.2 0.1 copy.23
  564.3 0.1 copy.24
  564.4 5.8 cholesky.81
  570.3 0.6 compare_reduce_fusion
  570.9 0.7 fusion.33
  571.6 4.9 custom-call.11
  576.5 0.2 fusion.36
  576.7 0.2 fusion.34
  576.9 2.1 fusion.1
  579.0 1.1 convolution_subtract_fusion
  580.1 1.1 convolution_add_fusion
  (19 shorter events, 0.3 us)
Async XLA Ops:
  7.2 9.7 %copy-start.1 = (s32[384]{0:T(512)S(1)}, s32[384]{0:T(512)}, u32[]{:S(2)}) copy-start(s32[384]{0:T(512)} %param.7) | copy-start | bytes 4612
  7.2 84.9 %reduce-scatter.4.cloned.1.call-start = ((), (), s32[]{:S(2)}) async-start(), calls=%async_computation.3 | async-start | bytes 4456448 | tf_op jit(solution)/shard_map/reduce_scatter | solution.py:37
  16.8 118.7 %all-gather.3.cloned.1.call-start = ((), (), s32[]{:S(2)}) async-start(), calls=%async_computation.4 | async-start | bytes 2228224 | tf_op jit(solution)/shard_map/all_gather | solution.py:51
  93.8 60.3 %copy-start = (f32[1024,64]{0,1:T(8,128)S(1)}, f32[1024,64]{0,1:T(8,128)}, u32[]{:S(2)}) copy-start(f32[1024,64]{0,1:T(8,128)} %reduce-scatter.4.cloned.1.call-done) | copy-start | bytes 786436
  93.8 131.5 %reduce-scatter.6.cloned.1.call-start = ((), (), s32[]{:S(2)}) async-start(), calls=%async_computation.5 | async-start | bytes 4456448 | tf_op jit(solution)/shard_map/reduce_scatter | solution.py:55
  154.0 258.9 %all-gather.5.cloned.1.call-start = ((), (), s32[]{:S(2)}) async-start(), calls=%async_computation.6 | async-start | bytes 2228224 | tf_op jit(solution)/shard_map/all_gather | solution.py:51
  374.1 128.7 %reduce-scatter.8.cloned.1.call-start = ((), (), s32[]{:S(2)}) async-start(), calls=%async_computation.7 | async-start | bytes 4456448 | tf_op jit(solution)/shard_map/reduce_scatter | solution.py:55
Sparse Core Ops, SparseCore 0:
  16.9 75.1 reduce-scatter.3
  95.1 40.4 all-gather.2
  154.1 71.1 reduce-scatter.5
  374.2 38.6 all-gather.4
  431.5 71.2 reduce-scatter.7
where the time goes:
time: 588 us
  waiting for transfers between devices  260 us (44%)
  blocking collectives  211 us (36%)
  matrix products  62 us (11%)
  other arithmetic  39.4 us (7%)
  between operations  14.1 us (2%)
    reduce_scatter x2, waiting for transfers between devices, per_device(): lax.psum_scatter(contract_rows(activations, weighted), 'dp', scatter_dime...  140 us
    psum x2, blocking collectives, per_device(): lax.psum((precise(class_means.T, direction), precise(direction.T, panel),...  118 us
    all_gather x2, waiting for transfers between devices, per_device(): lax.all_gather(direction.astype(jnp.bfloat16), 'dp', axis=0, tiled=True)  80.2 us
    psum x1, blocking collectives, per_device(): renewed = symmetric(lax.psum(precise(residual.T, residual), 'dp'))  57.6 us
    dot_general x3, matrix products, contract_rows(): lax.dot_general(left_side, right_side, (((0,), (0,)), ((), ())), preferre...  45.8 us
    reduce_scatter x1, waiting for transfers between devices, per_device(): lax.psum_scatter(contract_rows(activations, member), 'dp', scatter_dimens...  39.5 us
    psum x1, blocking collectives, per_device(): class_weight = lax.psum(local_weight, 'dp')  35 us
    another operation x9, other arithmetic, solve_positive(): jnp.linalg.cholesky(matrix)  19.6 us
  transfers between devices with their start and end apart: 5, of which 5 were waited for; matrix products, arithmetic and copies ran while one was open for 0% of the time, Pallas kernels for 0%

commit v1 on v0

--- a/solution.py
+++ b/solution.py
@@ -73,7 +73,9 @@
         residual = residual - precise(image, step_alpha)
         renewed = current
         if iteration + 1 < ITERS:
-            renewed = symmetric(lax.psum(precise(residual.T, residual), "dp"))
+            renewed = symmetric(
+                jnp.sum(lax.all_gather(precise(residual.T, residual), "dp"), axis=0)
+            )
         if iteration + 1 < ITERS:
             step_beta = solve_positive(current, renewed)
             direction = residual + precise(direction, step_beta)

time: 588 us -> 551 us (0.937)
  blocking collectives: 211 us -> 172 us
    psum x1 -> x0, blocking collectives: 57.6 us -> none  [per_device(): renewed = symmetric(lax.psum(precise(residual.T, residual), 'dp'))]
    all_gather x0 -> x1, blocking collectives: none -> 18.7 us  [per_device(): lax.all_gather(precise(residual.T, residual), 'dp')]
  transfers between devices with their start and end apart: 5 -> 5, of which waited for: 5 -> 5; matrix products, arithmetic and copies ran while one was open for 0% -> 1% of each run, Pallas kernels for 0% -> 0%
where the time goes in v1:
time: 551 us
  waiting for transfers between devices  262 us (48%)
  blocking collectives  172 us (31%)
  matrix products  62 us (11%)
  other arithmetic  39.4 us (7%)
  between operations  14.1 us (3%)
    reduce_scatter x2, waiting for transfers between devices, per_device(): lax.psum_scatter(contract_rows(activations, weighted), 'dp', scatter_dime...  140 us
    psum x2, blocking collectives, per_device(): lax.psum((precise(class_means.T, direction), precise(direction.T, panel),...  118 us
    all_gather x2, waiting for transfers between devices, per_device(): lax.all_gather(direction.astype(jnp.bfloat16), 'dp', axis=0, tiled=True)  82.1 us
    dot_general x3, matrix products, contract_rows(): lax.dot_general(left_side, right_side, (((0,), (0,)), ((), ())), preferre...  45.8 us
    reduce_scatter x1, waiting for transfers between devices, per_device(): lax.psum_scatter(contract_rows(activations, member), 'dp', scatter_dimens...  39.5 us
    psum x1, blocking collectives, per_device(): class_weight = lax.psum(local_weight, 'dp')  35 us
    another operation x9, other arithmetic, solve_positive(): jnp.linalg.cholesky(matrix)  19.6 us
    all_gather x1, blocking collectives, per_device(): lax.all_gather(precise(residual.T, residual), 'dp')  18.7 us
  transfers between devices with their start and end apart: 5, of which 5 were waited for; matrix products, arithmetic and copies ran while one was open for 1% of the time, Pallas kernels for 0%

profile of v1, /device:TPU:0, one launch (start us, length us, event | category | flops | bytes accessed | tf_op | source)
XLA Modules:
  0.0 550.8 jit_solution(4039987608946947404)
XLA Ops:
  7.2 0.0 reduce-scatter.4.cloned.1.call-start
  7.2 0.7 convert_element_type.20
  7.9 8.9 %convolution_bitcast_fusion.2 = f32[16384,64]{0,1:T(8,128)} fusion(bf16[384,16384]{1,0:T(8,128)(2,1)} %param.6, f32[384]{0:T(512)S(1)} %convert_element_type.20, s32[384]{0:T(512)} %param.7), kind=kOutput, calls=%fused_computation.2 | convolution fusion | flops 805355520 | bytes 16780288 | tf_op jit(solution)/shard_map/dot_general | solution.py:26
  16.8 0.0 all-gather.4.cloned.1.call-start
  16.8 0.1 select_reduce_fusion
  17.0 35.0 %psum.52 = f32[64]{0:T(128)S(1)} all-reduce(f32[64]{0:T(128)S(1)} %select_reduce_fusion), channel_id=1, replica_groups=mesh['groups'=2,'dp'=16] {'dp'}, use_global_device_ids=true, to_apply=%region_2.3 | all-reduce | flops 64 | bytes 512 | tf_op jit(solution)/shard_map/psum | solution.py:40
  52.0 0.6 fusion.62
  52.6 39.5 %reduce-scatter.4.cloned.1.call-done = f32[1024,64]{0,1:T(8,128)} async-done(((f32[16384,64]{0,1:T(8,128)}), f32[1024,64]{0,1:T(8,128)}) %reduce-scatter.4.cloned.1.call-update) | async-done | bytes 262160 | tf_op jit(solution)/shard_map/reduce_scatter | solution.py:37
  92.1 1.7 multiply_convert_fusion
  93.8 0.0 reduce-scatter.6.cloned.1.call-start
  93.9 41.7 %all-gather.4.cloned.1.call-done = bf16[16384,64]{0,1:T(8,128)(2,1)} async-done(((bf16[1024,64]{0,1:T(8,128)(2,1)}), bf16[16384,64]{0,1:T(8,128)(2,1)}) %all-gather.4.cloned.1.call-update) | async-done | bytes 2097168 | tf_op jit(solution)/shard_map/all_gather | solution.py:51
  135.5 18.5 %convolution_bitcast_fusion.1 = f32[16384,64]{0,1:T(8,128)} fusion(bf16[384,16384]{1,0:T(8,128)(2,1)} %param.6, bf16[16384,64]{0,1:T(8,128)(2,1)} %all-gather.4.cloned.1.call-done, f32[384]{0:T(512)S(1)} %convert_element_type.20), kind=kOutput, calls=%fused_computation.1 | convolution fusion | flops 1610661888 | bytes 18875904 | tf_op jit(solution)/shard_map/dot_general | solution.py:26
  154.0 0.0 all-gather.6.cloned.1.call-start
  154.1 0.5 fusion.13
  154.5 0.5 fusion.15
  155.0 70.3 %reduce-scatter.6.cloned.1.call-done = f32[1024,64]{0,1:T(8,128)} async-done(((f32[16384,64]{0,1:T(8,128)}), f32[1024,64]{0,1:T(8,128)}) %reduce-scatter.6.cloned.1.call-update) | async-done | bytes 262160 | tf_op jit(solution)/shard_map/reduce_scatter | solution.py:55
  225.3 1.4 fusion.17
  226.7 59.2 %all-reduce.1 = (f32[64,64]{1,0:T(8,128)S(1)}, f32[64,64]{1,0:T(8,128)S(1)}, f32[64,64]{1,0:T(8,128)S(1)}) all-reduce(f32[64,64]{1,0:T(8,128)S(1)} %fusion.13, f32[64,64]{1,0:T(8,128)S(1)} %fusion.17, f32[64,64]{1,0:T(8,128)S(1)} %fusion.15), channel_id=1, replica_groups=mesh['groups'=2,'dp'=16] {'dp'}, use_global_device_ids=true, to_apply=%region_7.8 | all-reduce | flops 12288 | bytes 98304 | tf_op jit(solution)/shard_map/psum | solution.py:58
  285.9 0.1 copy.19
  286.0 0.9 fusion.9
  286.9 0.1 copy.15
  287.0 0.1 copy.17
  287.1 0.1 copy.18
  287.2 5.9 %cholesky.59 = f32[64,64]{1,0:T(8,128)S(1)} custom-call(f32[64,64]{1,0:T(8,128)S(1)} %copy.18), custom_call_target="Cholesky" | custom-call | tf_op jit(solution)/shard_map/jit(cholesky)/cholesky | solution.py:22
  293.1 0.6 compare_reduce_fusion.2
  293.7 0.7 fusion.31
  294.4 4.9 custom-call.9
  299.3 0.1 copy.20
  299.4 0.2 fusion.48
  299.6 0.2 fusion.46
  299.8 2.1 fusion.3
  301.9 0.4 convolution_subtract_fusion.2
  302.3 0.4 fusion.64
  302.7 18.7 %all-gather = f32[1024,64]{1,0:T(8,128)S(1)} all-gather(f32[64,64]{1,0:T(8,128)S(1)} %fusion.64), channel_id=2, replica_groups=mesh['groups'=2,'dp'=16] {'dp'}, dimensions={0}, use_global_device_ids=true | all-gather | bytes 278528 | tf_op jit(solution)/shard_map/all_gather | solution.py:77
  321.4 0.1 copy.21
  321.5 5.8 %cholesky.70 = f32[64,64]{1,0:T(8,128)S(1)} custom-call(f32[64,64]{1,0:T(8,128)S(1)} %fusion.44), custom_call_target="Cholesky" | custom-call | tf_op jit(solution)/shard_map/jit(cholesky)/cholesky | solution.py:22
  327.4 0.6 compare_reduce_fusion.1
  328.1 0.7 fusion.32
  328.7 4.9 custom-call.10
  333.6 0.2 fusion.42
  333.9 0.2 fusion.40
  334.0 1.1 fusion.63
  335.2 0.3 reduce-scatter.8.cloned.1.call-start
  335.4 40.4 %all-gather.6.cloned.1.call-done = bf16[16384,64]{0,1:T(8,128)(2,1)} async-done(((bf16[1024,64]{0,1:T(8,128)(2,1)}), bf16[16384,64]{0,1:T(8,128)(2,1)}) %all-gather.6.cloned.1.call-update) | async-done | bytes 2097168 | tf_op jit(solution)/shard_map/all_gather | solution.py:51
  375.9 18.5 %convolution_bitcast_fusion = f32[16384,64]{0,1:T(8,128)} fusion(bf16[384,16384]{1,0:T(8,128)(2,1)} %param.6, bf16[16384,64]{0,1:T(8,128)(2,1)} %all-gather.6.cloned.1.call-done, f32[384]{0:T(512)S(1)} %convert_element_type.20), kind=kOutput, calls=%fused_computation | convolution fusion | flops 1610661888 | bytes 18875904 | tf_op jit(solution)/shard_map/dot_general | solution.py:26
  394.4 0.4 fusion.66
  394.7 0.4 fusion.61
  395.2 0.5 fusion.11
  395.6 70.1 %reduce-scatter.8.cloned.1.call-done = f32[1024,64]{0,1:T(8,128)} async-done(((f32[16384,64]{0,1:T(8,128)}), f32[1024,64]{0,1:T(8,128)}) %reduce-scatter.8.cloned.1.call-update) | async-done | bytes 262160 | tf_op jit(solution)/shard_map/reduce_scatter | solution.py:55
  465.8 1.3 fusion.65
  467.1 59.1 %all-reduce = (f32[64,64]{1,0:T(8,128)S(1)}, f32[64,64]{1,0:T(8,128)S(1)}, f32[64,64]{1,0:T(8,128)S(1)}) all-reduce(f32[64,64]{1,0:T(8,128)S(1)} %fusion.65, f32[64,64]{1,0:T(8,128)S(1)} %fusion.61, f32[64,64]{1,0:T(8,128)S(1)} %fusion.66), channel_id=1, replica_groups=mesh['groups'=2,'dp'=16] {'dp'}, use_global_device_ids=true, to_apply=%region_12.15 | all-reduce | flops 12288 | bytes 98304 | tf_op jit(solution)/shard_map/psum | solution.py:58
  526.2 0.9 fusion.7
  527.1 0.1 copy.22
  527.2 0.1 copy.23
  527.3 0.1 copy.24
  527.4 5.8 %cholesky.81 = f32[64,64]{1,0:T(8,128)S(1)} custom-call(f32[64,64]{1,0:T(8,128)S(1)} %fusion.38), custom_call_target="Cholesky" | custom-call | tf_op jit(solution)/shard_map/jit(cholesky)/cholesky | solution.py:22
  533.2 0.6 compare_reduce_fusion
  533.9 0.7 fusion.33
  534.6 4.9 custom-call.11
  539.4 0.2 fusion.36
  539.7 0.2 fusion.34
  539.9 2.1 fusion.1
  542.0 1.1 convolution_subtract_fusion
  543.1 1.1 convolution_add_fusion
  (20 shorter events, 0.3 us)
Async XLA Ops:
  7.2 9.7 %copy-start.1 = (s32[384]{0:T(512)S(1)}, s32[384]{0:T(512)}, u32[]{:S(2)}) copy-start(s32[384]{0:T(512)} %param.7) | copy-start | bytes 4612
  7.2 84.9 %reduce-scatter.4.cloned.1.call-start = ((), (), s32[]{:S(2)}) async-start(), calls=%async_computation.3 | async-start | bytes 4456448 | tf_op jit(solution)/shard_map/reduce_scatter | solution.py:37
  16.8 118.7 %all-gather.4.cloned.1.call-start = ((), (), s32[]{:S(2)}) async-start(), calls=%async_computation.4 | async-start | bytes 2228224 | tf_op jit(solution)/shard_map/all_gather | solution.py:51
  93.8 60.3 %copy-start = (f32[1024,64]{0,1:T(8,128)S(1)}, f32[1024,64]{0,1:T(8,128)}, u32[]{:S(2)}) copy-start(f32[1024,64]{0,1:T(8,128)} %reduce-scatter.4.cloned.1.call-done) | copy-start | bytes 786436
  93.8 131.5 %reduce-scatter.6.cloned.1.call-start = ((), (), s32[]{:S(2)}) async-start(), calls=%async_computation.5 | async-start | bytes 4456448 | tf_op jit(solution)/shard_map/reduce_scatter | solution.py:55
  154.0 221.9 %all-gather.6.cloned.1.call-start = ((), (), s32[]{:S(2)}) async-start(), calls=%async_computation.6 | async-start | bytes 2228224 | tf_op jit(solution)/shard_map/all_gather | solution.py:51
  335.2 130.6 %reduce-scatter.8.cloned.1.call-start = ((), (), s32[]{:S(2)}) async-start(), calls=%async_computation.7 | async-start | bytes 4456448 | tf_op jit(solution)/shard_map/reduce_scatter | solution.py:55
Sparse Core Ops, SparseCore 0:
  16.9 75.1 reduce-scatter.3
  95.1 40.4 all-gather.3
  154.1 71.1 reduce-scatter.5
  335.3 40.5 all-gather.5
  394.5 71.2 reduce-scatter.7
